TPU v7x, 512 devices: a whole 4x4x16 slice. The times are simulated.
512 devices in a mesh: ctx: 128 (over z, x_hi, y), tp: 4 (over x_lo, core).
Axes of the slice: x: 4 (x_hi: 2, x_lo: 2; x = x_hi * 2 + x_lo), y: 4, z: 16, core: 2. Of those that a mesh axis runs over, the one named last changes fastest.
Arguments:
- streams: bfloat16 [3, 256, 16384], P(None, 'tp', 'ctx'), may hold values from -6 to 6
- filter_raw: float32 [256, 16384], P('tp', 'ctx'), may hold values from -6 to 6
- grad_output: bfloat16 [256, 16384], P('tp', 'ctx'), may hold values from -6 to 6
Outputs:
- mixed_out: bfloat16 [256, 16384], P('tp', 'ctx')
- grad_streams: bfloat16 [3, 256, 16384], P(None, 'tp', 'ctx')
- grad_filter: float32 [256, 16384], P('tp', 'ctx')
All inputs are finite; a program needn't handle non-finite values.
Results may differ from a plain program's by a relative error of at most 0.0014.
Values sent between devices are 32-bit elements; how exact they have to be, the bound alone decides.
A program may use at most 64 MiB of HBM per device.

v0:
```python
import math

import jax
import jax.numpy as jnp
import numpy as np
from jax import lax
from jax.experimental import pallas as pl
from jax.experimental.pallas import tpu as pltpu
from jax.sharding import PartitionSpec as P

MESH = pl.DeviceIdType.MESH
BARRIER = "full"


def split_table(table):
    high = table.astype(jnp.bfloat16)
    low = (table - high.astype(np.float64)).astype(jnp.bfloat16)
    return high, low


def make_tables(rows, lanes):
    length = 2 * rows * lanes
    place = np.arange(rows, dtype=np.int64)
    twice = 2 * np.arange(rows, dtype=np.int64) + 1
    column = np.arange(lanes, dtype=np.int64)
    angle = 2.0 * np.pi / (4 * rows) * (twice[:, None] * place[None, :] % (4 * rows))
    outer = np.concatenate([np.cos(angle), -np.sin(angle)], axis=0)
    angle = 2.0 * np.pi / lanes * (column[:, None] * column[None, :] % lanes)
    cosine, sine = np.cos(angle), np.sin(angle)
    inner = np.block([[cosine, -sine], [sine, cosine]])
    angle = 2.0 * np.pi / (2 * length) * (twice[:, None] * column[None, :] % (2 * length))
    twist = np.stack([np.cos(angle), np.sin(angle)]).astype(np.float32)
    scale = 2.0 / length
    tables = []
    for table in (outer, inner, inner.T, outer.T * scale):
        tables.extend(split_table(table))
    return tables + [twist]


def split_value(value):
    high = value.astype(jnp.bfloat16)
    low = (value - high.astype(jnp.float32)).astype(jnp.bfloat16)
    return high, low


def dot(left, right):
    return jnp.dot(left, right, preferred_element_type=jnp.float32)


def table_times(high, low, value):
    value_high, value_low = split_value(value)
    return dot(high[...], value_high) + (dot(high[...], value_low) + dot(low[...], value_high))


def times_table(value, high, low):
    value_high, value_low = split_value(value)
    return dot(value_high, high[...]) + (dot(value_low, high[...]) + dot(value_high, low[...]))


def far_first(step, count):
    half = count // 2
    back = (step + 1) // 2
    return lax.select(lax.rem(step, 2) == 0, half - back, half + back)


def kernel(
    devices,
    tap_scale,
    streams_ref,
    filter_ref,
    grad_ref,
    *refs,
):
    tables_hbm = refs[:9]
    mixed_ref, grads_ref, taps_ref = refs[9:12]
    outgoing, arrived, results, returned = refs[12:16]
    tables = refs[16:25]
    (table_sem, out_send, out_recv, back_send, back_recv, self_sem) = refs[25:]
    channels, lanes = filter_ref.shape
    me = lax.axis_index("ctx")
    tp = lax.axis_index("tp")
    spread = devices // channels
    core = lax.rem(tp, spread)
    mine = me // spread
    owner = lax.rem(me, spread) == core

    barrier = pltpu.get_barrier_semaphore()

    @pl.loop(1, devices)
    def _(step):
        peer = lax.rem(me + step, devices)
        pl.semaphore_signal(barrier, inc=1, device_id=(peer, tp), device_id_type=MESH)

    loads = [
        pltpu.make_async_copy(source, target, table_sem.at[at])
        for at, (source, target) in enumerate(zip(tables_hbm, tables))
    ]
    for load in loads:
        load.start()

    query = streams_ref[0].astype(jnp.float32)
    key = streams_ref[1].astype(jnp.float32)
    value = streams_ref[2].astype(jnp.float32)
    upstream = grad_ref[...].astype(jnp.float32)
    outgoing[:, 0, 0:lanes] = key * value
    outgoing[:, 0, lanes : 2 * lanes] = filter_ref[...] * tap_scale
    outgoing[:, 0, 2 * lanes : 3 * lanes] = query * upstream

    pl.semaphore_wait(barrier, devices - 1)

    def send_out(channel):
        return pltpu.make_async_remote_copy(
            src_ref=outgoing.at[channel],
            dst_ref=arrived.at[me],
            send_sem=out_send,
            recv_sem=out_recv,
            device_id=(channel * spread + core, tp),
            device_id_type=MESH,
        )

    def keep(source, target):
        return pltpu.make_async_copy(source, target, self_sem)

    @pl.loop(0, channels - 1)
    def _(step):
        send_out(lax.rem(mine + far_first(step, channels), channels)).start()

    @pl.when(jnp.logical_not(owner))
    def _():
        send_out(mine).start()

    @pl.when(owner)
    def _():
        keep(outgoing.at[mine], arrived.at[me]).start()
        keep(outgoing.at[mine], arrived.at[me]).wait()

    for load in loads:
        load.wait()

    outer_high, outer_low, inner_high, inner_low = tables[:4]
    back_high, back_low, final_high, final_low, twist = tables[4:]

    def send_back(target):
        return pltpu.make_async_remote_copy(
            src_ref=results.at[target],
            dst_ref=returned.at[mine],
            send_sem=back_send,
            recv_sem=back_recv,
            device_id=(target, tp),
            device_id_type=MESH,
        )

    def block_copy(block, send_sem, recv_sem):
        return pltpu.make_async_remote_copy(
            src_ref=block,
            dst_ref=block,
            send_sem=send_sem,
            recv_sem=recv_sem,
            device_id=(lax.rem(me + 1, devices), tp),
            device_id_type=MESH,
        )

    @pl.when(owner)
    def _():
        block_copy(arrived.at[pl.ds(0, devices - 1)], out_send, out_recv).wait_recv()
        cosine, sine = twist[0], twist[1]
        signal = jnp.concatenate(
            [arrived[:, 0, at * lanes : (at + 1) * lanes] for at in range(3)], axis=1
        )
        rows = table_times(outer_high, outer_low, signal)
        spectra = []
        for at in range(3):
            real = rows[:devices, at * lanes : (at + 1) * lanes]
            imag = rows[devices:, at * lanes : (at + 1) * lanes]
            turned = jnp.concatenate(
                [real * cosine + imag * sine, imag * cosine - real * sine], axis=1
            )
            both = times_table(turned, inner_high, inner_low)
            spectra.append((both[:, :lanes], both[:, lanes:]))
        (gated_r, gated_i), (taps_r, taps_i), (grad_r, grad_i) = spectra
        products = (
            (gated_r * taps_r - gated_i * taps_i, gated_r * taps_i + gated_i * taps_r),
            (grad_r * taps_r + grad_i * taps_i, grad_i * taps_r - grad_r * taps_i),
            (grad_r * gated_r + grad_i * gated_i, grad_i * gated_r - grad_r * gated_i),
        )
        columns = []
        for real, imag in products:
            both = times_table(jnp.concatenate([real, imag], axis=1), back_high, back_low)
            real, imag = both[:, :lanes], both[:, lanes:]
            columns.append(
                jnp.concatenate([real * cosine - imag * sine, imag * cosine + real * sine], axis=0)
            )
        final = table_times(final_high, final_low, jnp.concatenate(columns, axis=1))
        for at in range(3):
            results[:, 0, at * lanes : (at + 1) * lanes] = final[:, at * lanes : (at + 1) * lanes]

        @pl.loop(0, devices - 1)
        def _(step):
            send_back(lax.rem(me + far_first(step, devices), devices)).start()

        keep(results.at[me], returned.at[mine]).start()
        keep(results.at[me], returned.at[mine]).wait()
        block_copy(returned.at[pl.ds(0, channels - 1)], back_send, back_recv).wait_recv()
        block_copy(outgoing.at[pl.ds(0, channels - 1)], out_send, out_recv).wait_send()

    @pl.when(jnp.logical_not(owner))
    def _():
        block_copy(returned, back_send, back_recv).wait_recv()
        block_copy(outgoing, out_send, out_recv).wait_send()

    long_conv = returned[:, 0, 0:lanes]
    grad_gated = returned[:, 0, lanes : 2 * lanes]
    mixed_ref[...] = (streams_ref[0].astype(jnp.float32) * long_conv).astype(jnp.bfloat16)
    grads_ref[0] = (grad_ref[...].astype(jnp.float32) * long_conv).astype(jnp.bfloat16)
    grads_ref[1] = (grad_gated * streams_ref[2].astype(jnp.float32)).astype(jnp.bfloat16)
    grads_ref[2] = (grad_gated * streams_ref[1].astype(jnp.float32)).astype(jnp.bfloat16)
    taps_ref[...] = returned[:, 0, 2 * lanes : 3 * lanes] * tap_scale

    @pl.when(owner)
    def _():
        block_copy(results.at[pl.ds(0, devices - 1)], back_send, back_recv).wait_send()


def local(devices, streams, filter_raw, grad_output):
    channels, lanes = filter_raw.shape
    tap_scale = 1.0 / math.sqrt(lanes * devices)
    tables = [jnp.asarray(table) for table in make_tables(devices, lanes)]
    vmem = pl.BlockSpec(memory_space=pltpu.VMEM)
    hbm = pl.BlockSpec(memory_space=pl.ANY)
    width = 3 * lanes
    import functools

    return pl.pallas_call(
        functools.partial(kernel, devices, tap_scale),
        out_shape=(
            jax.ShapeDtypeStruct((channels, lanes), jnp.bfloat16),
            jax.ShapeDtypeStruct((3, channels, lanes), jnp.bfloat16),
            jax.ShapeDtypeStruct((channels, lanes), jnp.float32),
        ),
        in_specs=[vmem] * 3 + [hbm] * len(tables),
        out_specs=(vmem, vmem, vmem),
        scratch_shapes=[
            pltpu.VMEM((channels, 1, width), jnp.float32),
            pltpu.VMEM((devices, 1, width), jnp.float32),
            pltpu.VMEM((devices, 1, width), jnp.float32),
            pltpu.VMEM((channels, 1, width), jnp.float32),
        ]
        + [pltpu.VMEM(table.shape, table.dtype) for table in tables]
        + [pltpu.SemaphoreType.DMA((len(tables),))]
        + [pltpu.SemaphoreType.DMA] * 5,
        compiler_params=pltpu.CompilerParams(
            collective_id=0, has_side_effects=True, vmem_limit_bytes=32 << 20
        ),
    )(streams, filter_raw, grad_output, *tables)


def solution(mesh):
    devices = mesh.shape["ctx"]
    in_specs = (P(None, "tp", "ctx"), P("tp", "ctx"), P("tp", "ctx"))
    out_specs = (P("tp", "ctx"), P(None, "tp", "ctx"), P("tp", "ctx"))

    def program(streams, filter_raw, grad_output):
        return local(devices, streams, filter_raw, grad_output)

    return jax.shard_map(
        program, mesh=mesh, in_specs=in_specs, out_specs=out_specs, check_vma=False
    )
```

profile of v0, /device:TPU:2, one launch (start us, length us, event | category | flops | bytes accessed | tf_op | source)
XLA Modules:
  0.0 54.4 jit_solution(8853100541288619237)
XLA Ops:
  0.6 0.0 copy-start
  0.6 0.9 %copy-done = f32[2,128,128]{2,1,0:T(8,128)S(1)} copy-done((f32[2,128,128]{2,1,0:T(8,128)S(1)}, f32[2,128,128]{2,1,0:T(8,128)}, u32[]{:S(2)}) %copy-start) | copy-done | bytes 131096
  1.5 0.0 copy-start.1
  1.5 0.9 %copy-done.1 = bf16[256,256]{1,0:T(8,128)(2,1)S(1)} copy-done((bf16[256,256]{1,0:T(8,128)(2,1)S(1)}, bf16[256,256]{1,0:T(8,128)(2,1)}, u32[]{:S(2)}) %copy-start.1) | copy-done | bytes 131096
  2.4 0.0 copy-start.2
  2.4 0.9 %copy-done.2 = bf16[256,256]{1,0:T(8,128)(2,1)S(1)} copy-done((bf16[256,256]{1,0:T(8,128)(2,1)S(1)}, bf16[256,256]{1,0:T(8,128)(2,1)}, u32[]{:S(2)}) %copy-start.2) | copy-done | bytes 131096
  3.3 0.0 copy-start.3
  3.4 0.9 %copy-done.3 = bf16[256,256]{1,0:T(8,128)(2,1)S(1)} copy-done((bf16[256,256]{1,0:T(8,128)(2,1)S(1)}, bf16[256,256]{1,0:T(8,128)(2,1)}, u32[]{:S(2)}) %copy-start.3) | copy-done | bytes 131096
  4.3 0.0 copy-start.4
  4.3 0.9 %copy-done.4 = bf16[256,256]{1,0:T(8,128)(2,1)S(1)} copy-done((bf16[256,256]{1,0:T(8,128)(2,1)S(1)}, bf16[256,256]{1,0:T(8,128)(2,1)}, u32[]{:S(2)}) %copy-start.4) | copy-done | bytes 131096
  5.2 0.0 copy-start.5
  5.2 0.8 %copy-done.5 = bf16[128,256]{1,0:T(8,128)(2,1)S(1)} copy-done((bf16[128,256]{1,0:T(8,128)(2,1)S(1)}, bf16[128,256]{1,0:T(8,128)(2,1)}, u32[]{:S(2)}) %copy-start.5) | copy-done | bytes 65560
  6.0 0.0 copy-start.6
  6.0 0.8 %copy-done.6 = bf16[128,256]{1,0:T(8,128)(2,1)S(1)} copy-done((bf16[128,256]{1,0:T(8,128)(2,1)S(1)}, bf16[128,256]{1,0:T(8,128)(2,1)}, u32[]{:S(2)}) %copy-start.6) | copy-done | bytes 65560
  6.8 0.0 copy-start.7
  6.8 0.8 %copy-done.7 = bf16[256,128]{1,0:T(8,128)(2,1)S(1)} copy-done((bf16[256,128]{1,0:T(8,128)(2,1)S(1)}, bf16[256,128]{1,0:T(8,128)(2,1)}, u32[]{:S(2)}) %copy-start.7) | copy-done | bytes 65560
  7.7 0.0 copy-start.8
  7.7 0.8 %copy-done.8 = bf16[256,128]{1,0:T(8,128)(2,1)S(1)} copy-done((bf16[256,128]{1,0:T(8,128)(2,1)S(1)}, bf16[256,128]{1,0:T(8,128)(2,1)}, u32[]{:S(2)}) %copy-start.8) | copy-done | bytes 65560
  8.5 0.0 copy-start.9
  8.5 0.8 %copy-done.9 = bf16[3,64,128]{2,1,0:T(8,128)(2,1)S(1)} copy-done((bf16[3,64,128]{2,1,0:T(8,128)(2,1)S(1)}, bf16[3,64,128]{2,1,0:T(8,128)(2,1)}, u32[]{:S(2)}) %copy-start.9) | copy-done | bytes 49176
  9.3 0.0 copy-start.10
  9.3 0.8 %copy-done.10 = f32[64,128]{1,0:T(8,128)S(1)} copy-done((f32[64,128]{1,0:T(8,128)S(1)}, f32[64,128]{1,0:T(8,128)}, u32[]{:S(2)}) %copy-start.10) | copy-done | bytes 32792
  10.1 0.0 copy-start.11
  10.1 0.7 %copy-done.11 = bf16[64,128]{1,0:T(8,128)(2,1)S(1)} copy-done((bf16[64,128]{1,0:T(8,128)(2,1)S(1)}, bf16[64,128]{1,0:T(8,128)(2,1)}, u32[]{:S(2)}) %copy-start.11) | copy-done | bytes 16408
  10.8 41.8 %shard_map.139 = (bf16[64,128]{1,0:T(8,128)(2,1)S(1)}, bf16[3,64,128]{2,1,0:T(8,128)(2,1)S(1)}, f32[64,128]{1,0:T(8,128)S(1)}) custom-call(bf16[3,64,128]{2,1,0:T(8,128)(2,1)S(1)} %copy-done.9, f32[64,128]{1,0:T(8,128)S(1)} %copy-done.10, bf16[64,128]{1,0:T(8,128)(2,1)S(1)} %copy-done.11, bf16[256,128]{1,0:T(8,128)(2,1)S(1)} %copy-done.8, ...), custom_call_target="tpu_custom_call" | custom-call | tf_op jit(solution)/shard_map/pallas_call | solution.py:233
  52.6 0.6 %copy.18 = bf16[64,128]{1,0:T(8,128)(2,1)} copy(bf16[64,128]{1,0:T(8,128)(2,1)S(1)} %get-tuple-element.6) | data formatting | bytes 32768
  53.2 0.6 %copy.19 = bf16[3,64,128]{2,1,0:T(8,128)(2,1)} copy(bf16[3,64,128]{2,1,0:T(8,128)(2,1)S(1)} %get-tuple-element.7) | data formatting | bytes 98304
  53.8 0.6 %copy.20 = f32[64,128]{1,0:T(8,128)} copy(f32[64,128]{1,0:T(8,128)S(1)} %get-tuple-element.8) | data formatting | bytes 65536
Async XLA Ops:
  0.6 0.9 %copy-start = (f32[2,128,128]{2,1,0:T(8,128)S(1)}, f32[2,128,128]{2,1,0:T(8,128)}, u32[]{:S(2)}) copy-start(f32[2,128,128]{2,1,0:T(8,128)} %constant.26.clone.refs_8_) | copy-start | bytes 393220
  1.5 0.9 %copy-start.1 = (bf16[256,256]{1,0:T(8,128)(2,1)S(1)}, bf16[256,256]{1,0:T(8,128)(2,1)}, u32[]{:S(2)}) copy-start(bf16[256,256]{1,0:T(8,128)(2,1)} %constant.23.clone.refs_5_) | copy-start | bytes 393220
  2.4 0.9 %copy-start.2 = (bf16[256,256]{1,0:T(8,128)(2,1)S(1)}, bf16[256,256]{1,0:T(8,128)(2,1)}, u32[]{:S(2)}) copy-start(bf16[256,256]{1,0:T(8,128)(2,1)} %constant.22.clone.refs_4_) | copy-start | bytes 393220
  3.3 0.9 %copy-start.3 = (bf16[256,256]{1,0:T(8,128)(2,1)S(1)}, bf16[256,256]{1,0:T(8,128)(2,1)}, u32[]{:S(2)}) copy-start(bf16[256,256]{1,0:T(8,128)(2,1)} %constant.21.clone.refs_3_) | copy-start | bytes 393220
  4.3 0.9 %copy-start.4 = (bf16[256,256]{1,0:T(8,128)(2,1)S(1)}, bf16[256,256]{1,0:T(8,128)(2,1)}, u32[]{:S(2)}) copy-start(bf16[256,256]{1,0:T(8,128)(2,1)} %constant.20.clone.refs_2_) | copy-start | bytes 393220
  5.2 0.8 %copy-start.5 = (bf16[128,256]{1,0:T(8,128)(2,1)S(1)}, bf16[128,256]{1,0:T(8,128)(2,1)}, u32[]{:S(2)}) copy-start(bf16[128,256]{1,0:T(8,128)(2,1)} %constant.25.clone.refs_7_) | copy-start | bytes 196612
  6.0 0.8 %copy-start.6 = (bf16[128,256]{1,0:T(8,128)(2,1)S(1)}, bf16[128,256]{1,0:T(8,128)(2,1)}, u32[]{:S(2)}) copy-start(bf16[128,256]{1,0:T(8,128)(2,1)} %constant.24.clone.refs_6_) | copy-start | bytes 196612
  6.8 0.8 %copy-start.7 = (bf16[256,128]{1,0:T(8,128)(2,1)S(1)}, bf16[256,128]{1,0:T(8,128)(2,1)}, u32[]{:S(2)}) copy-start(bf16[256,128]{1,0:T(8,128)(2,1)} %constant.19.clone.refs_1_) | copy-start | bytes 196612
  7.7 0.8 %copy-start.8 = (bf16[256,128]{1,0:T(8,128)(2,1)S(1)}, bf16[256,128]{1,0:T(8,128)(2,1)}, u32[]{:S(2)}) copy-start(bf16[256,128]{1,0:T(8,128)(2,1)} %constant.18.clone.refs_0_) | copy-start | bytes 196612
  8.5 0.8 %copy-start.9 = (bf16[3,64,128]{2,1,0:T(8,128)(2,1)S(1)}, bf16[3,64,128]{2,1,0:T(8,128)(2,1)}, u32[]{:S(2)}) copy-start(bf16[3,64,128]{2,1,0:T(8,128)(2,1)} %streams_ref.1) | copy-start | bytes 147460
  9.3 0.8 %copy-start.10 = (f32[64,128]{1,0:T(8,128)S(1)}, f32[64,128]{1,0:T(8,128)}, u32[]{:S(2)}) copy-start(f32[64,128]{1,0:T(8,128)} %filter_ref.1) | copy-start | bytes 98308
  10.1 0.7 %copy-start.11 = (bf16[64,128]{1,0:T(8,128)(2,1)S(1)}, bf16[64,128]{1,0:T(8,128)(2,1)}, u32[]{:S(2)}) copy-start(bf16[64,128]{1,0:T(8,128)(2,1)} %grad_ref.1) | copy-start | bytes 49156
where the time goes:
time: 55 us; the launch traced here: 54.4 us
  Pallas kernels  41.8 us (76%)
  local copies, waits for them, and re-layouts  12 us (22%)
  between operations  0.66 us (1%)
    pallas_call x1, Pallas kernels, local(): pl.pallas_call(functools.partial(kernel, devices, tap_scale), out_shape=(...  41.8 us
    unnamed x27, local copies, waits for them, and re-layouts  12 us

commit v1 on v0

v1 whole, which is shorter than its diff:
```python
import functools
import math

import jax
import jax.numpy as jnp
import numpy as np
from jax import lax
from jax.experimental import pallas as pl
from jax.experimental.pallas import tpu as pltpu
from jax.sharding import PartitionSpec as P

MESH = pl.DeviceIdType.MESH
ACROSS = 4
FIRST = 4


def split_table(table):
    high = table.astype(jnp.bfloat16)
    low = (table - high.astype(np.float64)).astype(jnp.bfloat16)
    return high, low


def make_tables(rows, lanes):
    length = 2 * rows * lanes
    place = np.arange(rows, dtype=np.int64)
    twice = 2 * np.arange(rows, dtype=np.int64) + 1
    column = np.arange(lanes, dtype=np.int64)
    angle = 2.0 * np.pi / (4 * rows) * (twice[:, None] * place[None, :] % (4 * rows))
    outer = np.concatenate([np.cos(angle), -np.sin(angle)], axis=0)
    angle = 2.0 * np.pi / lanes * (column[:, None] * column[None, :] % lanes)
    cosine, sine = np.cos(angle), np.sin(angle)
    inner = np.block([[cosine, -sine], [sine, cosine]])
    angle = 2.0 * np.pi / (2 * length) * (twice[:, None] * column[None, :] % (2 * length))
    twist = np.stack([np.cos(angle), np.sin(angle)]).astype(np.float32)
    scale = 2.0 / length
    tables = []
    for table in (outer, inner, inner.T, outer.T * scale):
        tables.extend(split_table(table))
    return tables + [twist]


def split_value(value):
    high = value.astype(jnp.bfloat16)
    low = (value - high.astype(jnp.float32)).astype(jnp.bfloat16)
    return high, low


def dot(left, right):
    return jnp.dot(left, right, preferred_element_type=jnp.float32)


def table_times(high, low, value):
    value_high, value_low = split_value(value)
    return dot(high[...], value_high) + (dot(high[...], value_low) + dot(low[...], value_high))


def times_table(value, high, low):
    value_high, value_low = split_value(value)
    return dot(value_high, high[...]) + (dot(value_low, high[...]) + dot(value_high, low[...]))


def convolve(signal, tables, rows_count, lanes):
    outer_high, outer_low, inner_high, inner_low = tables[:4]
    back_high, back_low, final_high, final_low, twist = tables[4:]
    cosine, sine = twist[0], twist[1]
    rows = table_times(outer_high, outer_low, signal)
    spectra = []
    for at in range(3):
        real = rows[:rows_count, at * lanes : (at + 1) * lanes]
        imag = rows[rows_count:, at * lanes : (at + 1) * lanes]
        turned = jnp.concatenate([real * cosine + imag * sine, imag * cosine - real * sine], axis=1)
        both = times_table(turned, inner_high, inner_low)
        spectra.append((both[:, :lanes], both[:, lanes:]))
    (gated_r, gated_i), (taps_r, taps_i), (grad_r, grad_i) = spectra
    products = (
        (gated_r * taps_r - gated_i * taps_i, gated_r * taps_i + gated_i * taps_r),
        (grad_r * taps_r + grad_i * taps_i, grad_i * taps_r - grad_r * taps_i),
        (grad_r * gated_r + grad_i * gated_i, grad_i * gated_r - grad_r * gated_i),
    )
    columns = []
    for real, imag in products:
        both = times_table(jnp.concatenate([real, imag], axis=1), back_high, back_low)
        real, imag = both[:, :lanes], both[:, lanes:]
        columns.append(
            jnp.concatenate([real * cosine - imag * sine, imag * cosine + real * sine], axis=0)
        )
    return table_times(final_high, final_low, jnp.concatenate(columns, axis=1))


def kernel(devices, tap_scale, streams_hbm, filter_hbm, grad_hbm, *refs):
    tables_hbm = refs[:9]
    mixed_ref, grads_ref, taps_ref = refs[9:12]
    outgoing, arrived, results, returned = refs[12:16]
    tables = refs[16:25]
    streams_ref, filter_ref, grad_ref = refs[25:28]
    input_sem, table_sem, out_send, out_recv, back_send, back_recv, self_sem = refs[28:]
    channels, lanes = filter_ref.shape
    me = lax.axis_index("ctx")
    tp = lax.axis_index("tp")
    barrier = pltpu.get_barrier_semaphore()

    plane = ACROSS * 2
    planes = devices // plane
    zed = me // plane
    side = lax.rem(me, plane) // ACROSS
    why = lax.rem(me, ACROSS)
    whys = [lax.rem(why + turn, ACROSS) for turn in range(ACROSS)]
    sides = [side * ACROSS, (1 - side) * ACROSS]
    far_turns = (2, 1, 3, 0)
    spots = [sides[flip] + whys[turn] for turn in far_turns for flip in (1, 0)]

    parity = lax.rem(tp, 2)
    home = me // 2
    owner = lax.rem(me, 2) == parity
    level = why - lax.rem(why, 2) + parity
    mates = [
        (sides[flip] + lax.rem(level + turn, ACROSS)) // 2 for turn in (2, 0) for flip in (1, 0)
    ]

    def plane_of(step):
        half = planes // 2
        back = (step + 1) // 2
        jump = lax.select(lax.rem(step, 2) == 0, half - back, half + back)
        return lax.rem(zed + jump, planes) * plane

    @pl.when(owner)
    def _():
        def greet(peer):
            pl.semaphore_signal(barrier, inc=1, device_id=(peer, tp), device_id_type=MESH)

        @pl.loop(0, planes - 1)
        def _(step):
            start = plane_of(step)
            for spot in spots:
                greet(start + spot)

        for spot in spots[:-1]:
            greet(zed * plane + spot)

    inputs = [
        pltpu.make_async_copy(source, target, input_sem.at[at])
        for at, (source, target) in enumerate(
            zip((streams_hbm, filter_hbm, grad_hbm), (streams_ref, filter_ref, grad_ref))
        )
    ]
    loads = [
        pltpu.make_async_copy(source, target, table_sem.at[at])
        for at, (source, target) in enumerate(zip(tables_hbm, tables))
    ]
    for load in inputs + loads:
        load.start()
    for load in inputs:
        load.wait()
    query = streams_ref[0].astype(jnp.float32)
    key = streams_ref[1].astype(jnp.float32)
    value = streams_ref[2].astype(jnp.float32)
    upstream = grad_ref[...].astype(jnp.float32)
    outgoing[:, 0, 0:lanes] = key * value
    outgoing[:, 0, lanes : 2 * lanes] = filter_ref[...] * tap_scale
    outgoing[:, 0, 2 * lanes : 3 * lanes] = query * upstream
    for load in loads:
        load.wait()

    @pl.when(owner)
    def _():
        pl.semaphore_wait(barrier, channels - 1)

    @pl.when(jnp.logical_not(owner))
    def _():
        pl.semaphore_wait(barrier, channels)

    def send_out(number):
        pltpu.make_async_remote_copy(
            src_ref=outgoing.at[number],
            dst_ref=arrived.at[me],
            send_sem=out_send,
            recv_sem=out_recv,
            device_id=(number * 2 + parity, tp),
            device_id_type=MESH,
        ).start()

    def send_back(target):
        pltpu.make_async_remote_copy(
            src_ref=results.at[target],
            dst_ref=returned.at[home],
            send_sem=back_send,
            recv_sem=back_recv,
            device_id=(target, tp),
            device_id_type=MESH,
        ).start()

    def block_copy(block, send_sem, recv_sem):
        return pltpu.make_async_remote_copy(
            src_ref=block,
            dst_ref=block,
            send_sem=send_sem,
            recv_sem=recv_sem,
            device_id=(lax.rem(me + 1, devices), tp),
            device_id_type=MESH,
        )

    def keep(source, target):
        copy = pltpu.make_async_copy(source, target, self_sem)
        copy.start()
        copy.wait()

    @pl.loop(0, planes - 1)
    def _(step):
        start = plane_of(step) // 2
        for mate in mates:
            send_out(start + mate)

    for mate in mates[:-1]:
        send_out(zed * (plane // 2) + mate)

    @pl.when(jnp.logical_not(owner))
    def _():
        send_out(home)

    @pl.when(owner)
    def _():
        keep(outgoing.at[home], arrived.at[me])
        block_copy(arrived.at[pl.ds(0, devices - 1)], out_send, out_recv).wait_recv()
        signal = jnp.concatenate(
            [arrived[:, 0, at * lanes : (at + 1) * lanes] for at in range(3)], axis=1
        )
        final = convolve(signal, tables, devices, lanes)
        for at in range(3):
            results[:, 0, at * lanes : (at + 1) * lanes] = final[:, at * lanes : (at + 1) * lanes]

        def back_plane(start):
            for spot in spots:
                send_back(start + spot)

        @pl.loop(0, FIRST)
        def _(step):
            number = lax.rem(zed + step, FIRST)

            @pl.when(number != zed)
            def _():
                back_plane(number * plane)

        @pl.loop(0, planes - 1)
        def _(step):
            start = plane_of(step)

            @pl.when(start >= FIRST * plane)
            def _():
                back_plane(start)

        for spot in spots[:-1]:
            send_back(zed * plane + spot)
        keep(results.at[me], returned.at[home])
        block_copy(returned.at[pl.ds(0, channels - 1)], back_send, back_recv).wait_recv()

    @pl.when(jnp.logical_not(owner))
    def _():
        block_copy(returned, back_send, back_recv).wait_recv()

    long_conv = returned[:, 0, 0:lanes]
    grad_gated = returned[:, 0, lanes : 2 * lanes]
    mixed_ref[...] = (streams_ref[0].astype(jnp.float32) * long_conv).astype(jnp.bfloat16)
    grads_ref[0] = (grad_ref[...].astype(jnp.float32) * long_conv).astype(jnp.bfloat16)
    grads_ref[1] = (grad_gated * streams_ref[2].astype(jnp.float32)).astype(jnp.bfloat16)
    grads_ref[2] = (grad_gated * streams_ref[1].astype(jnp.float32)).astype(jnp.bfloat16)
    taps_ref[...] = returned[:, 0, 2 * lanes : 3 * lanes] * tap_scale

    @pl.when(owner)
    def _():
        block_copy(outgoing.at[pl.ds(0, channels - 1)], out_send, out_recv).wait_send()
        block_copy(results.at[pl.ds(0, devices - 1)], back_send, back_recv).wait_send()

    @pl.when(jnp.logical_not(owner))
    def _():
        block_copy(outgoing, out_send, out_recv).wait_send()


def local(devices, streams, filter_raw, grad_output):
    channels, lanes = filter_raw.shape
    tap_scale = 1.0 / math.sqrt(lanes * devices)
    tables = [jnp.asarray(table) for table in make_tables(devices, lanes)]
    vmem = pl.BlockSpec(memory_space=pltpu.VMEM)
    anywhere = pl.BlockSpec(memory_space=pl.ANY)
    width = 3 * lanes
    inputs = (streams, filter_raw, grad_output)
    operands = [pltpu.with_memory_space_constraint(x, pltpu.HBM) for x in (*inputs, *tables)]
    return pl.pallas_call(
        functools.partial(kernel, devices, tap_scale),
        out_shape=(
            jax.ShapeDtypeStruct((channels, lanes), jnp.bfloat16),
            jax.ShapeDtypeStruct((3, channels, lanes), jnp.bfloat16),
            jax.ShapeDtypeStruct((channels, lanes), jnp.float32),
        ),
        in_specs=[anywhere] * len(operands),
        out_specs=(vmem, vmem, vmem),
        scratch_shapes=[
            pltpu.VMEM((channels, 1, width), jnp.float32),
            pltpu.VMEM((devices, 1, width), jnp.float32),
            pltpu.VMEM((devices, 1, width), jnp.float32),
            pltpu.VMEM((channels, 1, width), jnp.float32),
        ]
        + [pltpu.VMEM(table.shape, table.dtype) for table in tables]
        + [pltpu.VMEM(x.shape, x.dtype) for x in inputs]
        + [pltpu.SemaphoreType.DMA((3,)), pltpu.SemaphoreType.DMA((len(tables),))]
        + [pltpu.SemaphoreType.DMA] * 5,
        compiler_params=pltpu.CompilerParams(
            collective_id=0, has_side_effects=True, vmem_limit_bytes=32 << 20
        ),
    )(*operands)


def solution(mesh):
    devices = mesh.shape["ctx"]
    in_specs = (P(None, "tp", "ctx"), P("tp", "ctx"), P("tp", "ctx"))
    out_specs = (P("tp", "ctx"), P(None, "tp", "ctx"), P("tp", "ctx"))

    def program(streams, filter_raw, grad_output):
        return local(devices, streams, filter_raw, grad_output)

    return jax.shard_map(
        program, mesh=mesh, in_specs=in_specs, out_specs=out_specs, check_vma=False
    )
```

time: 55 us -> 41.8 us (0.76)
  local copies, waits for them, and re-layouts: 12 us -> 1.84 us
  Pallas kernels: 41.8 us -> 39.2 us
    unnamed x27 -> x3, local copies, waits for them, and re-layouts: 12 us -> 1.84 us
    pallas_call x1, Pallas kernels: 41.8 us -> 39.2 us  [local(): pl.pallas_call(functools.partial(kernel, devices, tap_scale), out_shape=(...]
where the time goes in v1:
time: 41.8 us; the launch traced here: 41.7 us
  Pallas kernels  39.2 us (94%)
  local copies, waits for them, and re-layouts  1.84 us (4%)
  between operations  0.64 us (2%)
    pallas_call x1, Pallas kernels, local(): pl.pallas_call(functools.partial(kernel, devices, tap_scale), out_shape=(...  39.2 us
    unnamed x3, local copies, waits for them, and re-layouts  1.84 us

profile of v1, /device:TPU:2, one launch (start us, length us, event | category | flops | bytes accessed | tf_op | source)
XLA Modules:
  0.0 41.7 jit_solution(7171589812592920013)
XLA Ops:
  0.6 39.2 %shard_map.139 = (bf16[64,128]{1,0:T(8,128)(2,1)S(1)}, bf16[3,64,128]{2,1,0:T(8,128)(2,1)S(1)}, f32[64,128]{1,0:T(8,128)S(1)}) custom-call(bf16[3,64,128]{2,1,0:T(8,128)(2,1)} %streams_hbm.1, f32[64,128]{1,0:T(8,128)} %filter_hbm.1, bf16[64,128]{1,0:T(8,128)(2,1)} %grad_hbm.1, bf16[256,128]{1,0:T(8,128)(2,1)} %constant.18.clone.refs_0_, ...), custom_call_target="tpu_custom_call" | custom-call | tf_op jit(solution)/shard_map/pallas_call | solution.py:287
  39.9 0.6 %copy.18 = bf16[64,128]{1,0:T(8,128)(2,1)} copy(bf16[64,128]{1,0:T(8,128)(2,1)S(1)} %get-tuple-element.6) | data formatting | bytes 32768
  40.5 0.6 %copy.19 = bf16[3,64,128]{2,1,0:T(8,128)(2,1)} copy(bf16[3,64,128]{2,1,0:T(8,128)(2,1)S(1)} %get-tuple-element.7) | data formatting | bytes 98304
  41.1 0.6 %copy.20 = f32[64,128]{1,0:T(8,128)} copy(f32[64,128]{1,0:T(8,128)S(1)} %get-tuple-element.8) | data formatting | bytes 65536

commit v2 on v1

--- a/solution.py
+++ b/solution.py
@@ -93,7 +93,7 @@
     outgoing, arrived, results, returned = refs[12:16]
     tables = refs[16:25]
     streams_ref, filter_ref, grad_ref = refs[25:28]
-    input_sem, table_sem, out_send, out_recv, back_send, back_recv, self_sem = refs[28:]
+    input_sem, table_sem, out_send, out_recv, back_send, back_recv = refs[28:]
     channels, lanes = filter_ref.shape
     me = lax.axis_index("ctx")
     tp = lax.axis_index("tp")
@@ -110,8 +110,11 @@
     spots = [sides[flip] + whys[turn] for turn in far_turns for flip in (1, 0)]
 
     parity = lax.rem(tp, 2)
+    across_x = 2 * (1 - tp // 2)
+    keeper = across_x + 1
+    served = across_x + lax.rem(me, 2)
     home = me // 2
-    owner = lax.rem(me, 2) == parity
+    owner = parity == 1
     level = why - lax.rem(why, 2) + parity
     mates = [
         (sides[flip] + lax.rem(level + turn, ACROSS)) // 2 for turn in (2, 0) for flip in (1, 0)
@@ -126,16 +129,13 @@
     @pl.when(owner)
     def _():
         def greet(peer):
-            pl.semaphore_signal(barrier, inc=1, device_id=(peer, tp), device_id_type=MESH)
-
-        @pl.loop(0, planes - 1)
+            pl.semaphore_signal(barrier, inc=1, device_id=(peer, served), device_id_type=MESH)
+
+        @pl.loop(0, planes)
         def _(step):
             start = plane_of(step)
             for spot in spots:
                 greet(start + spot)
-
-        for spot in spots[:-1]:
-            greet(zed * plane + spot)
 
     inputs = [
         pltpu.make_async_copy(source, target, input_sem.at[at])
@@ -161,13 +161,7 @@
     for load in loads:
         load.wait()
 
-    @pl.when(owner)
-    def _():
-        pl.semaphore_wait(barrier, channels - 1)
-
-    @pl.when(jnp.logical_not(owner))
-    def _():
-        pl.semaphore_wait(barrier, channels)
+    pl.semaphore_wait(barrier, channels)
 
     def send_out(number):
         pltpu.make_async_remote_copy(
@@ -175,7 +169,7 @@
             dst_ref=arrived.at[me],
             send_sem=out_send,
             recv_sem=out_recv,
-            device_id=(number * 2 + parity, tp),
+            device_id=(number * 2 + parity, keeper),
             device_id_type=MESH,
         ).start()
 
@@ -185,7 +179,7 @@
             dst_ref=returned.at[home],
             send_sem=back_send,
             recv_sem=back_recv,
-            device_id=(target, tp),
+            device_id=(target, served),
             device_id_type=MESH,
         ).start()
 
@@ -195,32 +189,19 @@
             dst_ref=block,
             send_sem=send_sem,
             recv_sem=recv_sem,
-            device_id=(lax.rem(me + 1, devices), tp),
+            device_id=(me, across_x),
             device_id_type=MESH,
         )
 
-    def keep(source, target):
-        copy = pltpu.make_async_copy(source, target, self_sem)
-        copy.start()
-        copy.wait()
-
-    @pl.loop(0, planes - 1)
+    @pl.loop(0, planes)
     def _(step):
         start = plane_of(step) // 2
         for mate in mates:
             send_out(start + mate)
 
-    for mate in mates[:-1]:
-        send_out(zed * (plane // 2) + mate)
-
-    @pl.when(jnp.logical_not(owner))
-    def _():
-        send_out(home)
-
     @pl.when(owner)
     def _():
-        keep(outgoing.at[home], arrived.at[me])
-        block_copy(arrived.at[pl.ds(0, devices - 1)], out_send, out_recv).wait_recv()
+        block_copy(arrived, out_send, out_recv).wait_recv()
         signal = jnp.concatenate(
             [arrived[:, 0, at * lanes : (at + 1) * lanes] for at in range(3)], axis=1
         )
@@ -234,13 +215,9 @@
 
         @pl.loop(0, FIRST)
         def _(step):
-            number = lax.rem(zed + step, FIRST)
-
-            @pl.when(number != zed)
-            def _():
-                back_plane(number * plane)
-
-        @pl.loop(0, planes - 1)
+            back_plane(lax.rem(zed + step, FIRST) * plane)
+
+        @pl.loop(0, planes)
         def _(step):
             start = plane_of(step)
 
@@ -248,15 +225,7 @@
             def _():
                 back_plane(start)
 
-        for spot in spots[:-1]:
-            send_back(zed * plane + spot)
-        keep(results.at[me], returned.at[home])
-        block_copy(returned.at[pl.ds(0, channels - 1)], back_send, back_recv).wait_recv()
-
-    @pl.when(jnp.logical_not(owner))
-    def _():
-        block_copy(returned, back_send, back_recv).wait_recv()
-
+    block_copy(returned, back_send, back_recv).wait_recv()
     long_conv = returned[:, 0, 0:lanes]
     grad_gated = returned[:, 0, lanes : 2 * lanes]
     mixed_ref[...] = (streams_ref[0].astype(jnp.float32) * long_conv).astype(jnp.bfloat16)
@@ -265,14 +234,11 @@
     grads_ref[2] = (grad_gated * streams_ref[1].astype(jnp.float32)).astype(jnp.bfloat16)
     taps_ref[...] = returned[:, 0, 2 * lanes : 3 * lanes] * tap_scale
 
+    block_copy(outgoing, out_send, out_recv).wait_send()
+
     @pl.when(owner)
     def _():
-        block_copy(outgoing.at[pl.ds(0, channels - 1)], out_send, out_recv).wait_send()
-        block_copy(results.at[pl.ds(0, devices - 1)], back_send, back_recv).wait_send()
-
-    @pl.when(jnp.logical_not(owner))
-    def _():
-        block_copy(outgoing, out_send, out_recv).wait_send()
+        block_copy(results, back_send, back_recv).wait_send()
 
 
 def local(devices, streams, filter_raw, grad_output):
@@ -302,7 +268,7 @@
         + [pltpu.VMEM(table.shape, table.dtype) for table in tables]
         + [pltpu.VMEM(x.shape, x.dtype) for x in inputs]
         + [pltpu.SemaphoreType.DMA((3,)), pltpu.SemaphoreType.DMA((len(tables),))]
-        + [pltpu.SemaphoreType.DMA] * 5,
+        + [pltpu.SemaphoreType.DMA] * 4,
         compiler_params=pltpu.CompilerParams(
             collective_id=0, has_side_effects=True, vmem_limit_bytes=32 << 20
         ),

time: 41.8 us -> 41 us (0.981)
  the two profiles are of different devices: /device:TPU:2 before, /device:TPU:1 now
where the time goes in v2:
time: 41 us; the launch traced here: 40.9 us
  Pallas kernels  38.4 us (94%)
  local copies, waits for them, and re-layouts  1.84 us (4%)
  between operations  0.64 us (2%)
    pallas_call x1, Pallas kernels, local(): pl.pallas_call(functools.partial(kernel, devices, tap_scale), out_shape=(...  38.4 us
    unnamed x3, local copies, waits for them, and re-layouts  1.84 us

profile of v2, /device:TPU:1, one launch (start us, length us, event | category | flops | bytes accessed | tf_op | source)
XLA Modules:
  0.0 40.9 jit_solution(4021714400224485134)
XLA Ops:
  0.6 38.4 %shard_map.139 = (bf16[64,128]{1,0:T(8,128)(2,1)S(1)}, bf16[3,64,128]{2,1,0:T(8,128)(2,1)S(1)}, f32[64,128]{1,0:T(8,128)S(1)}) custom-call(bf16[3,64,128]{2,1,0:T(8,128)(2,1)} %streams_hbm.1, f32[64,128]{1,0:T(8,128)} %filter_hbm.1, bf16[64,128]{1,0:T(8,128)(2,1)} %grad_hbm.1, bf16[256,128]{1,0:T(8,128)(2,1)} %constant.18.clone.refs_0_, ...), custom_call_target="tpu_custom_call" | custom-call | tf_op jit(solution)/shard_map/pallas_call | solution.py:253
  39.0 0.6 %copy.18 = bf16[64,128]{1,0:T(8,128)(2,1)} copy(bf16[64,128]{1,0:T(8,128)(2,1)S(1)} %get-tuple-element.6) | data formatting | bytes 32768
  39.7 0.6 %copy.19 = bf16[3,64,128]{2,1,0:T(8,128)(2,1)} copy(bf16[3,64,128]{2,1,0:T(8,128)(2,1)S(1)} %get-tuple-element.7) | data formatting | bytes 98304
  40.3 0.6 %copy.20 = f32[64,128]{1,0:T(8,128)} copy(f32[64,128]{1,0:T(8,128)S(1)} %get-tuple-element.8) | data formatting | bytes 65536

commit v3 on v2

--- a/solution.py
+++ b/solution.py
@@ -241,6 +241,17 @@
         block_copy(results, back_send, back_recv).wait_send()
 
 
+def store_kernel(*refs):
+    copies = [
+        pltpu.make_async_copy(source, target, refs[-1].at[at])
+        for at, (source, target) in enumerate(zip(refs[:3], refs[3:6]))
+    ]
+    for copy in copies:
+        copy.start()
+    for copy in copies:
+        copy.wait()
+
+
 def local(devices, streams, filter_raw, grad_output):
     channels, lanes = filter_raw.shape
     tap_scale = 1.0 / math.sqrt(lanes * devices)
@@ -250,7 +261,7 @@
     width = 3 * lanes
     inputs = (streams, filter_raw, grad_output)
     operands = [pltpu.with_memory_space_constraint(x, pltpu.HBM) for x in (*inputs, *tables)]
-    return pl.pallas_call(
+    results = pl.pallas_call(
         functools.partial(kernel, devices, tap_scale),
         out_shape=(
             jax.ShapeDtypeStruct((channels, lanes), jnp.bfloat16),
@@ -273,6 +284,16 @@
             collective_id=0, has_side_effects=True, vmem_limit_bytes=32 << 20
         ),
     )(*operands)
+    results = [pltpu.with_memory_space_constraint(x, pltpu.VMEM) for x in results]
+    shapes = tuple(jax.ShapeDtypeStruct(x.shape, x.dtype) for x in results)
+    return pl.pallas_call(
+        store_kernel,
+        out_shape=shapes,
+        in_specs=[anywhere] * 3,
+        out_specs=[anywhere] * 3,
+        scratch_shapes=[pltpu.SemaphoreType.DMA((3,))],
+        compiler_params=pltpu.CompilerParams(vmem_limit_bytes=8 << 20),
+    )(*results)
 
 
 def solution(mesh):

time: 41 us -> 39.9 us (0.973)
  local copies, waits for them, and re-layouts: 1.84 us -> 0 us
  Pallas kernels: 38.4 us -> 39.1 us
    unnamed x3 -> x0, local copies, waits for them, and re-layouts: 1.84 us -> none
    pallas_call x0 -> x1, Pallas kernels: none -> 0.67 us  [local(): pl.pallas_call(store_kernel, out_shape=shapes, in_specs=[anywhere] * 3, o...]
where the time goes in v3:
time: 39.9 us; the launch traced here: 39.7 us
  Pallas kernels  39.1 us (98%)
  between operations  0.64 us (2%)
    pallas_call x1, Pallas kernels, local(): pl.pallas_call(functools.partial(kernel, devices, tap_scale), out_shape=(...  38.4 us

profile of v3, /device:TPU:1, one launch (start us, length us, event | category | flops | bytes accessed | tf_op | source)
XLA Modules:
  0.0 39.7 jit_solution(7676015274517701966)
XLA Ops:
  0.6 38.4 %shard_map.139 = (bf16[64,128]{1,0:T(8,128)(2,1)S(1)}, bf16[3,64,128]{2,1,0:T(8,128)(2,1)S(1)}, f32[64,128]{1,0:T(8,128)S(1)}) custom-call(bf16[3,64,128]{2,1,0:T(8,128)(2,1)} %streams_hbm.1, f32[64,128]{1,0:T(8,128)} %filter_hbm.1, bf16[64,128]{1,0:T(8,128)(2,1)} %grad_hbm.1, bf16[256,128]{1,0:T(8,128)(2,1)} %constant.18.clone.refs_0_, ...), custom_call_target="tpu_custom_call" | custom-call | tf_op jit(solution)/shard_map/pallas_call | solution.py:264
  39.0 0.7 %shard_map.140 = (bf16[64,128]{1,0:T(8,128)(2,1)}, bf16[3,64,128]{2,1,0:T(8,128)(2,1)}, f32[64,128]{1,0:T(8,128)}) custom-call(bf16[64,128]{1,0:T(8,128)(2,1)S(1)} %get-tuple-element.6.refs_0_, bf16[3,64,128]{2,1,0:T(8,128)(2,1)S(1)} %get-tuple-element.7.refs_1_, f32[64,128]{1,0:T(8,128)S(1)} %get-tuple-element.8.refs_2_), custom_call_target="tpu_custom_call" | custom-call | tf_op jit(solution)/shard_map/pallas_call | solution.py:289

commit v4 on v1

--- a/solution.py
+++ b/solution.py
@@ -109,13 +109,15 @@
     far_turns = (2, 1, 3, 0)
     spots = [sides[flip] + whys[turn] for turn in far_turns for flip in (1, 0)]
 
-    parity = lax.rem(tp, 2)
-    home = me // 2
-    owner = lax.rem(me, 2) == parity
-    level = why - lax.rem(why, 2) + parity
-    mates = [
-        (sides[flip] + lax.rem(level + turn, ACROSS)) // 2 for turn in (2, 0) for flip in (1, 0)
-    ]
+    core = lax.rem(tp, 2)
+    low = tp // 2
+    keeper = lax.select(core == 0, 3 - 2 * low, tp)
+    served = lax.select(side == low, tp, 2 - 2 * low)
+    home = zed * ACROSS + why
+    owner = core == 1
+    alone = jnp.logical_and(owner, side == low)
+    paired = jnp.logical_not(alone)
+    mates = [whys[turn] for turn in far_turns]
 
     def plane_of(step):
         half = planes // 2
@@ -126,7 +128,7 @@
     @pl.when(owner)
     def _():
         def greet(peer):
-            pl.semaphore_signal(barrier, inc=1, device_id=(peer, tp), device_id_type=MESH)
+            pl.semaphore_signal(barrier, inc=1, device_id=(peer, served), device_id_type=MESH)
 
         @pl.loop(0, planes - 1)
         def _(step):
@@ -136,6 +138,10 @@
 
         for spot in spots[:-1]:
             greet(zed * plane + spot)
+
+        @pl.when(paired)
+        def _():
+            greet(me)
 
     inputs = [
         pltpu.make_async_copy(source, target, input_sem.at[at])
@@ -155,37 +161,37 @@
     key = streams_ref[1].astype(jnp.float32)
     value = streams_ref[2].astype(jnp.float32)
     upstream = grad_ref[...].astype(jnp.float32)
-    outgoing[:, 0, 0:lanes] = key * value
-    outgoing[:, 0, lanes : 2 * lanes] = filter_ref[...] * tap_scale
-    outgoing[:, 0, 2 * lanes : 3 * lanes] = query * upstream
+    outgoing[0] = key * value
+    outgoing[1] = filter_ref[...] * tap_scale
+    outgoing[2] = query * upstream
     for load in loads:
         load.wait()
 
-    @pl.when(owner)
+    @pl.when(alone)
     def _():
         pl.semaphore_wait(barrier, channels - 1)
 
-    @pl.when(jnp.logical_not(owner))
+    @pl.when(paired)
     def _():
         pl.semaphore_wait(barrier, channels)
 
     def send_out(number):
         pltpu.make_async_remote_copy(
-            src_ref=outgoing.at[number],
-            dst_ref=arrived.at[me],
+            src_ref=outgoing.at[:, pl.ds(number, 1), :],
+            dst_ref=arrived.at[:, pl.ds(me, 1), :],
             send_sem=out_send,
             recv_sem=out_recv,
-            device_id=(number * 2 + parity, tp),
+            device_id=(number // ACROSS * plane + low * ACROSS + lax.rem(number, ACROSS), keeper),
             device_id_type=MESH,
         ).start()
 
     def send_back(target):
         pltpu.make_async_remote_copy(
-            src_ref=results.at[target],
-            dst_ref=returned.at[home],
+            src_ref=results.at[:, pl.ds(target, 1), :],
+            dst_ref=returned.at[:, pl.ds(home, 1), :],
             send_sem=back_send,
             recv_sem=back_recv,
-            device_id=(target, tp),
+            device_id=(target, served),
             device_id_type=MESH,
         ).start()
 
@@ -195,7 +201,7 @@
             dst_ref=block,
             send_sem=send_sem,
             recv_sem=recv_sem,
-            device_id=(lax.rem(me + 1, devices), tp),
+            device_id=(me, lax.rem(tp + 1, 4)),
             device_id_type=MESH,
         )
 
@@ -203,6 +209,11 @@
         copy = pltpu.make_async_copy(source, target, self_sem)
         copy.start()
         copy.wait()
+
+    mine = pl.ds(me, 1)
+    housed = pl.ds(home, 1)
+    most = pl.ds(0, devices - 1)
+    many = pl.ds(0, channels - 1)
 
     @pl.loop(0, planes - 1)
     def _(step):
@@ -211,22 +222,29 @@
             send_out(start + mate)
 
     for mate in mates[:-1]:
-        send_out(zed * (plane // 2) + mate)
-
-    @pl.when(jnp.logical_not(owner))
+        send_out(zed * ACROSS + mate)
+
+    @pl.when(paired)
     def _():
         send_out(home)
 
     @pl.when(owner)
     def _():
-        keep(outgoing.at[home], arrived.at[me])
-        block_copy(arrived.at[pl.ds(0, devices - 1)], out_send, out_recv).wait_recv()
+        @pl.when(alone)
+        def _():
+            keep(outgoing.at[:, housed, :], arrived.at[:, mine, :])
+            block_copy(arrived.at[:, most, :], out_send, out_recv).wait_recv()
+
+        @pl.when(paired)
+        def _():
+            block_copy(arrived, out_send, out_recv).wait_recv()
+
         signal = jnp.concatenate(
-            [arrived[:, 0, at * lanes : (at + 1) * lanes] for at in range(3)], axis=1
+            [arrived[at] for at in range(3)], axis=1
         )
         final = convolve(signal, tables, devices, lanes)
         for at in range(3):
-            results[:, 0, at * lanes : (at + 1) * lanes] = final[:, at * lanes : (at + 1) * lanes]
+            results[at] = final[:, at * lanes : (at + 1) * lanes]
 
         def back_plane(start):
             for spot in spots:
@@ -234,7 +252,8 @@
 
         @pl.loop(0, FIRST)
         def _(step):
-            number = lax.rem(zed + step, FIRST)
+            turn = lax.select(jnp.logical_and(alone, low == 1), 0, zed)
+            number = lax.rem(turn + step, FIRST)
 
             @pl.when(number != zed)
             def _():
@@ -250,29 +269,51 @@
 
         for spot in spots[:-1]:
             send_back(zed * plane + spot)
-        keep(results.at[me], returned.at[home])
-        block_copy(returned.at[pl.ds(0, channels - 1)], back_send, back_recv).wait_recv()
-
-    @pl.when(jnp.logical_not(owner))
+
+        @pl.when(paired)
+        def _():
+            send_back(me)
+
+    @pl.when(alone)
+    def _():
+        keep(results.at[:, mine, :], returned.at[:, housed, :])
+        block_copy(returned.at[:, many, :], back_send, back_recv).wait_recv()
+
+    @pl.when(paired)
     def _():
         block_copy(returned, back_send, back_recv).wait_recv()
 
-    long_conv = returned[:, 0, 0:lanes]
-    grad_gated = returned[:, 0, lanes : 2 * lanes]
+    long_conv = returned[0]
+    grad_gated = returned[1]
     mixed_ref[...] = (streams_ref[0].astype(jnp.float32) * long_conv).astype(jnp.bfloat16)
     grads_ref[0] = (grad_ref[...].astype(jnp.float32) * long_conv).astype(jnp.bfloat16)
     grads_ref[1] = (grad_gated * streams_ref[2].astype(jnp.float32)).astype(jnp.bfloat16)
     grads_ref[2] = (grad_gated * streams_ref[1].astype(jnp.float32)).astype(jnp.bfloat16)
-    taps_ref[...] = returned[:, 0, 2 * lanes : 3 * lanes] * tap_scale
-
-    @pl.when(owner)
-    def _():
-        block_copy(outgoing.at[pl.ds(0, channels - 1)], out_send, out_recv).wait_send()
-        block_copy(results.at[pl.ds(0, devices - 1)], back_send, back_recv).wait_send()
-
-    @pl.when(jnp.logical_not(owner))
+    taps_ref[...] = returned[2] * tap_scale
+
+    @pl.when(alone)
+    def _():
+        block_copy(outgoing.at[:, many, :], out_send, out_recv).wait_send()
+        block_copy(results.at[:, most, :], back_send, back_recv).wait_send()
+
+    @pl.when(paired)
     def _():
         block_copy(outgoing, out_send, out_recv).wait_send()
+
+    @pl.when(jnp.logical_and(owner, paired))
+    def _():
+        block_copy(results, back_send, back_recv).wait_send()
+
+
+def store_kernel(*refs):
+    copies = [
+        pltpu.make_async_copy(source, target, refs[-1].at[at])
+        for at, (source, target) in enumerate(zip(refs[:3], refs[3:6]))
+    ]
+    for copy in copies:
+        copy.start()
+    for copy in copies:
+        copy.wait()
 
 
 def local(devices, streams, filter_raw, grad_output):
@@ -281,10 +322,9 @@
     tables = [jnp.asarray(table) for table in make_tables(devices, lanes)]
     vmem = pl.BlockSpec(memory_space=pltpu.VMEM)
     anywhere = pl.BlockSpec(memory_space=pl.ANY)
-    width = 3 * lanes
     inputs = (streams, filter_raw, grad_output)
     operands = [pltpu.with_memory_space_constraint(x, pltpu.HBM) for x in (*inputs, *tables)]
-    return pl.pallas_call(
+    results = pl.pallas_call(
         functools.partial(kernel, devices, tap_scale),
         out_shape=(
             jax.ShapeDtypeStruct((channels, lanes), jnp.bfloat16),
@@ -294,10 +334,10 @@
         in_specs=[anywhere] * len(operands),
         out_specs=(vmem, vmem, vmem),
         scratch_shapes=[
-            pltpu.VMEM((channels, 1, width), jnp.float32),
-            pltpu.VMEM((devices, 1, width), jnp.float32),
-            pltpu.VMEM((devices, 1, width), jnp.float32),
-            pltpu.VMEM((channels, 1, width), jnp.float32),
+            pltpu.VMEM((3, channels, lanes), jnp.float32),
+            pltpu.VMEM((3, devices, lanes), jnp.float32),
+            pltpu.VMEM((3, devices, lanes), jnp.float32),
+            pltpu.VMEM((3, channels, lanes), jnp.float32),
         ]
         + [pltpu.VMEM(table.shape, table.dtype) for table in tables]
         + [pltpu.VMEM(x.shape, x.dtype) for x in inputs]
@@ -307,6 +347,16 @@
             collective_id=0, has_side_effects=True, vmem_limit_bytes=32 << 20
         ),
     )(*operands)
+    results = [pltpu.with_memory_space_constraint(x, pltpu.VMEM) for x in results]
+    shapes = tuple(jax.ShapeDtypeStruct(x.shape, x.dtype) for x in results)
+    return pl.pallas_call(
+        store_kernel,
+        out_shape=shapes,
+        in_specs=[anywhere] * 3,
+        out_specs=[anywhere] * 3,
+        scratch_shapes=[pltpu.SemaphoreType.DMA((3,))],
+        compiler_params=pltpu.CompilerParams(vmem_limit_bytes=8 << 20),
+    )(*results)
 
 
 def solution(mesh):

time: 41.8 us -> 38.7 us (0.926)
  the two profiles are of different devices: /device:TPU:2 before, /device:TPU:3 now
where the time goes in v4:
time: 38.7 us; the launch traced here: 38.5 us
  Pallas kernels  37.9 us (98%)
  between operations  0.64 us (2%)
    pallas_call x1, Pallas kernels, local(): pl.pallas_call(functools.partial(kernel, devices, tap_scale), out_shape=(...  37.2 us

profile of v4, /device:TPU:3, one launch (start us, length us, event | category | flops | bytes accessed | tf_op | source)
XLA Modules:
  0.0 38.5 jit_solution(10865002004074783294)
XLA Ops:
  0.6 37.2 %shard_map.139 = (bf16[64,128]{1,0:T(8,128)(2,1)S(1)}, bf16[3,64,128]{2,1,0:T(8,128)(2,1)S(1)}, f32[64,128]{1,0:T(8,128)S(1)}) custom-call(bf16[3,64,128]{2,1,0:T(8,128)(2,1)} %streams_hbm.1, f32[64,128]{1,0:T(8,128)} %filter_hbm.1, bf16[64,128]{1,0:T(8,128)(2,1)} %grad_hbm.1, bf16[256,128]{1,0:T(8,128)(2,1)} %constant.18.clone.refs_0_, ...), custom_call_target="tpu_custom_call" | custom-call | tf_op jit(solution)/shard_map/pallas_call | solution.py:327
  37.9 0.7 %shard_map.140 = (bf16[64,128]{1,0:T(8,128)(2,1)}, bf16[3,64,128]{2,1,0:T(8,128)(2,1)}, f32[64,128]{1,0:T(8,128)}) custom-call(bf16[64,128]{1,0:T(8,128)(2,1)S(1)} %get-tuple-element.6.refs_0_, bf16[3,64,128]{2,1,0:T(8,128)(2,1)S(1)} %get-tuple-element.7.refs_1_, f32[64,128]{1,0:T(8,128)S(1)} %get-tuple-element.8.refs_2_), custom_call_target="tpu_custom_call" | custom-call | tf_op jit(solution)/shard_map/pallas_call | solution.py:352

commit v5 on v4

--- a/solution.py
+++ b/solution.py
@@ -252,7 +252,7 @@
 
         @pl.loop(0, FIRST)
         def _(step):
-            turn = lax.select(jnp.logical_and(alone, low == 1), 0, zed)
+            turn = lax.select(low == 1, 0, zed)
             number = lax.rem(turn + step, FIRST)
 
             @pl.when(number != zed)

time: 38.7 us -> 38.7 us (level)
  no operation moved by 1% of the time
where the time goes in v5:
time: 38.7 us; the launch traced here: 38.5 us
  Pallas kernels  37.9 us (98%)
  between operations  0.64 us (2%)
    pallas_call x1, Pallas kernels, local(): pl.pallas_call(functools.partial(kernel, devices, tap_scale), out_shape=(...  37.2 us

profile of v5, /device:TPU:3, one launch (start us, length us, event | category | flops | bytes accessed | tf_op | source)
XLA Modules:
  0.0 38.5 jit_solution(10269801901815845940)
XLA Ops:
  0.6 37.2 %shard_map.139 = (bf16[64,128]{1,0:T(8,128)(2,1)S(1)}, bf16[3,64,128]{2,1,0:T(8,128)(2,1)S(1)}, f32[64,128]{1,0:T(8,128)S(1)}) custom-call(bf16[3,64,128]{2,1,0:T(8,128)(2,1)} %streams_hbm.1, f32[64,128]{1,0:T(8,128)} %filter_hbm.1, bf16[64,128]{1,0:T(8,128)(2,1)} %grad_hbm.1, bf16[256,128]{1,0:T(8,128)(2,1)} %constant.18.clone.refs_0_, ...), custom_call_target="tpu_custom_call" | custom-call | tf_op jit(solution)/shard_map/pallas_call | solution.py:327
  37.9 0.7 %shard_map.140 = (bf16[64,128]{1,0:T(8,128)(2,1)}, bf16[3,64,128]{2,1,0:T(8,128)(2,1)}, f32[64,128]{1,0:T(8,128)}) custom-call(bf16[64,128]{1,0:T(8,128)(2,1)S(1)} %get-tuple-element.6.refs_0_, bf16[3,64,128]{2,1,0:T(8,128)(2,1)S(1)} %get-tuple-element.7.refs_1_, f32[64,128]{1,0:T(8,128)S(1)} %get-tuple-element.8.refs_2_), custom_call_target="tpu_custom_call" | custom-call | tf_op jit(solution)/shard_map/pallas_call | solution.py:352

commit v6 on v4

--- a/solution.py
+++ b/solution.py
@@ -153,8 +153,14 @@
         pltpu.make_async_copy(source, target, table_sem.at[at])
         for at, (source, target) in enumerate(zip(tables_hbm, tables))
     ]
-    for load in inputs + loads:
+    for load in inputs:
         load.start()
+
+    @pl.when(owner)
+    def _():
+        for load in loads:
+            load.start()
+
     for load in inputs:
         load.wait()
     query = streams_ref[0].astype(jnp.float32)
@@ -164,9 +170,6 @@
     outgoing[0] = key * value
     outgoing[1] = filter_ref[...] * tap_scale
     outgoing[2] = query * upstream
-    for load in loads:
-        load.wait()
-
     @pl.when(alone)
     def _():
         pl.semaphore_wait(barrier, channels - 1)
@@ -230,6 +233,9 @@
 
     @pl.when(owner)
     def _():
+        for load in loads:
+            load.wait()
+
         @pl.when(alone)
         def _():
             keep(outgoing.at[:, housed, :], arrived.at[:, mine, :])

time: 38.7 us -> 38.7 us (level)
  no operation moved by 1% of the time
where the time goes in v6:
time: 38.7 us; the launch traced here: 38.5 us
  Pallas kernels  37.9 us (98%)
  between operations  0.64 us (2%)
    pallas_call x1, Pallas kernels, local(): pl.pallas_call(functools.partial(kernel, devices, tap_scale), out_shape=(...  37.2 us

profile of v6, /device:TPU:3, one launch (start us, length us, event | category | flops | bytes accessed | tf_op | source)
XLA Modules:
  0.0 38.5 jit_solution(14197110520844765896)
XLA Ops:
  0.6 37.2 %shard_map.139 = (bf16[64,128]{1,0:T(8,128)(2,1)S(1)}, bf16[3,64,128]{2,1,0:T(8,128)(2,1)S(1)}, f32[64,128]{1,0:T(8,128)S(1)}) custom-call(bf16[3,64,128]{2,1,0:T(8,128)(2,1)} %streams_hbm.1, f32[64,128]{1,0:T(8,128)} %filter_hbm.1, bf16[64,128]{1,0:T(8,128)(2,1)} %grad_hbm.1, bf16[256,128]{1,0:T(8,128)(2,1)} %constant.18.clone.refs_0_, ...), custom_call_target="tpu_custom_call" | custom-call | tf_op jit(solution)/shard_map/pallas_call | solution.py:333
  37.9 0.7 %shard_map.140 = (bf16[64,128]{1,0:T(8,128)(2,1)}, bf16[3,64,128]{2,1,0:T(8,128)(2,1)}, f32[64,128]{1,0:T(8,128)}) custom-call(bf16[64,128]{1,0:T(8,128)(2,1)S(1)} %get-tuple-element.6.refs_0_, bf16[3,64,128]{2,1,0:T(8,128)(2,1)S(1)} %get-tuple-element.7.refs_1_, f32[64,128]{1,0:T(8,128)S(1)} %get-tuple-element.8.refs_2_), custom_call_target="tpu_custom_call" | custom-call | tf_op jit(solution)/shard_map/pallas_call | solution.py:358

commit v7 on v5

--- a/solution.py
+++ b/solution.py
@@ -11,7 +11,7 @@
 
 MESH = pl.DeviceIdType.MESH
 ACROSS = 4
-FIRST = 4
+FIRST = 3
 
 
 def split_table(table):

time: 38.7 us -> 38.7 us (level)
  no operation moved by 1% of the time
where the time goes in v7:
time: 38.7 us; the launch traced here: 38.5 us
  Pallas kernels  37.9 us (98%)
  between operations  0.64 us (2%)
    pallas_call x1, Pallas kernels, local(): pl.pallas_call(functools.partial(kernel, devices, tap_scale), out_shape=(...  37.2 us

profile of v7, /device:TPU:3, one launch (start us, length us, event | category | flops | bytes accessed | tf_op | source)
XLA Modules:
  0.0 38.5 jit_solution(1896957368465349445)
XLA Ops:
  0.6 37.2 %shard_map.139 = (bf16[64,128]{1,0:T(8,128)(2,1)S(1)}, bf16[3,64,128]{2,1,0:T(8,128)(2,1)S(1)}, f32[64,128]{1,0:T(8,128)S(1)}) custom-call(bf16[3,64,128]{2,1,0:T(8,128)(2,1)} %streams_hbm.1, f32[64,128]{1,0:T(8,128)} %filter_hbm.1, bf16[64,128]{1,0:T(8,128)(2,1)} %grad_hbm.1, bf16[256,128]{1,0:T(8,128)(2,1)} %constant.18.clone.refs_0_, ...), custom_call_target="tpu_custom_call" | custom-call | tf_op jit(solution)/shard_map/pallas_call | solution.py:327
  37.9 0.7 %shard_map.140 = (bf16[64,128]{1,0:T(8,128)(2,1)}, bf16[3,64,128]{2,1,0:T(8,128)(2,1)}, f32[64,128]{1,0:T(8,128)}) custom-call(bf16[64,128]{1,0:T(8,128)(2,1)S(1)} %get-tuple-element.6.refs_0_, bf16[3,64,128]{2,1,0:T(8,128)(2,1)S(1)} %get-tuple-element.7.refs_1_, f32[64,128]{1,0:T(8,128)S(1)} %get-tuple-element.8.refs_2_), custom_call_target="tpu_custom_call" | custom-call | tf_op jit(solution)/shard_map/pallas_call | solution.py:352
